TPU v7x, 256 devices: a whole 4x4x8 slice. The times are simulated.
256 devices in a mesh: ctx: 32 (over x, z), head: 8 (over y, core).
Axes of the slice: x: 4, y: 4, z: 8, core: 2. Of those that a mesh axis runs over, the one named last changes fastest.
Arguments:
- queries: bfloat16 [8192, 32, 128], P('ctx', 'head'), may hold values from -40 to 40
- keys: bfloat16 [8192, 8, 128], P('ctx', 'head'), may hold values from -40 to 40
- values: bfloat16 [8192, 8, 128], P('ctx', 'head'), may hold values from -6 to 6
- doc_ids: int32 [8192], P('ctx'), may hold values from 0 to 3, never falling along the last dimension, each value on 1 to 4096 neighbouring positions
Outputs:
- attended: bfloat16 [8192, 4096], P(('ctx', 'head'))
Inputs may be any that keep to these rules, and one draw needn't show every extreme that they name: `doc_ids`: document numbers never fall along the sequence; each document has 1 to 4096 tokens and one has exactly 4096.
All inputs are finite; a program needn't handle non-finite values.
Results may differ from a plain program's by a relative error of at most 0.009.
Values may be sent and summed in bfloat16 or wider, within the bound.
No kernel may reach another device: no remote copies, remote signals or barrier semaphores. Data moves between devices by JAX's collectives and lax.ppermute only.
A program may use at most 128 MiB of HBM per device.

v0:
```python
import jax
import jax.numpy as jnp
from jax import lax
from jax.sharding import PartitionSpec as P


def attend(query_sets, keys, values, all_ids):
    kv_heads = keys.shape[1]
    head_dim = keys.shape[2]
    score_scale = head_dim ** (-0.5)
    prepared = []
    initial = []
    for query_rows, query_start in query_sets:
        row_count = query_rows.shape[0]
        q_heads = query_rows.shape[1]
        group_size = q_heads // kv_heads
        grouped = query_rows.reshape(row_count, kv_heads, group_size, head_dim)
        query_pos = query_start + jnp.arange(row_count, dtype=jnp.int32)
        query_ids = lax.dynamic_slice_in_dim(all_ids, query_start, row_count, 0)
        last_pos = query_start + row_count - 1
        prepared.append((grouped, query_pos, query_ids, last_pos))
        initial.append(
            (
                jnp.full((kv_heads, group_size, row_count), -1e30, jnp.float32),
                jnp.zeros((kv_heads, group_size, row_count), jnp.float32),
                jnp.zeros((kv_heads, group_size, row_count, head_dim), jnp.float32),
            )
        )
    carried = tuple(initial)
    key_start = jnp.int32(0)
    key_piece = lax.all_gather(keys, "ctx", axis=0, tiled=True)
    value_piece = lax.all_gather(values, "ctx", axis=0, tiled=True)
    piece_len = key_piece.shape[0]
    key_pos = jnp.arange(piece_len, dtype=jnp.int32)
    updated = []
    for (grouped, query_pos, query_ids, last_pos), state_now in zip(prepared, carried):

        def update(state_old, grouped=grouped, query_pos=query_pos, query_ids=query_ids):
            old_max, old_sum, accumulated = state_old
            scores = (
                jnp.einsum("nhgd,khd->hgnk", grouped, key_piece, preferred_element_type=jnp.float32)
                * score_scale
            )
            visible = (key_pos[None, :] <= query_pos[:, None]) & (
                all_ids[None, :] == query_ids[:, None]
            )
            scores = jnp.where(visible, scores, jnp.float32(-1e30))
            new_max = jnp.maximum(old_max, jnp.max(scores, axis=-1))
            weights = jnp.where(visible, jnp.exp(scores - new_max[..., None]), jnp.float32(0.0))
            new_sum = jnp.sum(weights, axis=-1)
            product = jnp.einsum(
                "hgnk,khd->hgnd",
                weights.astype(jnp.bfloat16),
                value_piece,
                preferred_element_type=jnp.float32,
            )
            return (new_max, new_sum, product)

        def unchanged(state_old):
            return state_old

        updated.append(lax.cond(key_start <= last_pos, update, unchanged, state_now))
    finals = tuple(updated)
    outputs = []
    for final_state in finals:
        run_max, run_sum, accumulated = final_state
        normed = accumulated / run_sum[..., None]
        row_count = normed.shape[2]
        joined = jnp.transpose(normed, (2, 0, 1, 3)).reshape(row_count, -1)
        outputs.append(joined.astype(jnp.bfloat16))
    return outputs


def local(queries, keys, values, doc_ids):
    tok_rows = queries.shape[0]
    ctx_place = lax.axis_index("ctx")
    all_ids = lax.all_gather(doc_ids, "ctx", axis=0, tiled=True)
    results = attend([(queries, ctx_place * tok_rows)], keys, values, all_ids)
    merged = results[0]
    return lax.all_to_all(merged, "head", split_axis=0, concat_axis=1, tiled=True)


def solution(mesh):
    return jax.shard_map(
        local,
        mesh=mesh,
        in_specs=(P("ctx", "head", None), P("ctx", "head", None), P("ctx", "head", None), P("ctx")),
        out_specs=P(("ctx", "head"), None),
        check_vma=False,
    )
```

profile of v0, /device:TPU:1, one launch (start us, length us, event | category | flops | bytes accessed | tf_op | source)
XLA Modules:
  0.0 239.5 jit_solution(13473183504084923722)
XLA Ops:
  6.5 0.0 all-gather.4.cloned.1.call-start
  6.5 0.7 all-gather.4.cloned.1.call-update
  7.3 0.0 all-gather.6.cloned.1.call-start
  7.3 0.7 all-gather.6.cloned.1.call-update
  8.0 37.9 %all-gather = s32[32,1,256]{2,1,0:T(1,128)S(1)} all-gather(s32[1,1,256]{2,1,0:T(1,128)} %bitcast.51), channel_id=1, replica_groups=mesh['ctx'=32,'head'=8] {'ctx'}, dimensions={0}, use_global_device_ids=true | all-gather | bytes 33792 | tf_op jit(solution)/shard_map/all_gather | solution.py:77
  46.0 41.1 %all-gather.4.cloned.1.call-done = bf16[8192,1,128]{2,0,1:T(8,128)(2,1)} async-done(((bf16[256,1,128]{2,0,1:T(8,128)(2,1)}), bf16[8192,1,128]{2,0,1:T(8,128)(2,1)}) %all-gather.4.cloned.1.call-update) | async-done | bytes 2097168 | tf_op jit(solution)/shard_map/all_gather | solution.py:31
  87.0 77.7 %all-gather.6.cloned.1.call-done = bf16[8192,1,128]{2,0,1:T(8,128)(2,1)} async-done(((bf16[256,1,128]{2,0,1:T(8,128)(2,1)}), bf16[8192,1,128]{2,0,1:T(8,128)(2,1)}) %all-gather.6.cloned.1.call-update) | async-done | bytes 2097168 | tf_op jit(solution)/shard_map/all_gather | solution.py:32
  164.7 50.8 %conditional.1 = (f32[1,4,256]{2,1,0:T(4,128)S(1)}, f32[1,4,256,128]{3,2,1,0:T(8,128)S(1)}) conditional(s32[]{:T(128)} %convert_element_type.17, () %tuple.16, (s32[8192]{0:T(1024)S(1)}, s32[]{:T(128)}, s32[256]{0:T(256)S(1)}, s32[8192]{0:T(1024)S(1)}, bf16[8192,1,128]{2,0,1:T(8,128)(2,1)}, /*index=5*/bf16[256,4,128]{2,1,0:T(4,128)(2,1)}, ...), branch_computations={%region_0.0_spmd, %region_1.4_spmd} | conditional | flops 4410309632 | bytes 122517592 | solution.py:62
  164.7 0.0 copy-start
  164.8 0.1 dynamic_slice.4
  164.8 5.6 %compare_and_fusion = pred[256,8192]{0,1:T(8,128)(4,1)S(1)} fusion(s32[256]{0:T(256)S(1)} %dynamic_slice.4, s32[256]{0:T(256)S(1)} %broadcast_add_fusion, s32[8192]{0:T(1024)S(1)} %get-tuple-element.58, s32[8192]{0:T(1024)S(1)} %get-tuple-element.55), kind=kLoop, calls=%fused_computation.8 | loop fusion | flops 6291456 | bytes 2164736 | tf_op jit(solution)/shard_map/cond/branch_1_fun/and | solution.py:44
  170.5 14.7 %fusion = (f32[4,256]{1,0:T(4,128)S(1)}, f32[8192,256,4]{1,0,2:T(8,128)}) fusion(pred[256,8192]{0,1:T(8,128)(4,1)S(1)} %compare_and_fusion, bf16[256,4,128]{2,1,0:T(4,128)(2,1)} %get-tuple-element.94, bf16[8192,1,128]{2,0,1:T(8,128)(2,1)} %get-tuple-element.59), kind=kOutput, calls=%fused_computation.2 | convolution fusion | flops 2172648448 | bytes 38014976 | tf_op jit(solution)/shard_map/cond/branch_1_fun/nhgd,khd->hgnk/dot_general | solution.py:41
  185.2 0.0 copy-done
  185.2 15.2 %fusion.10 = f32[1,4,256,128]{3,2,1,0:T(8,128)S(1)} fusion(bf16[8192,1,128]{2,0,1:T(8,128)(2,1)S(1)} %copy-done, f32[8192,256,4]{1,0,2:T(8,128)} %get-tuple-element.97, f32[4,256]{1,0:T(4,128)S(1)} %broadcast_maximum_fusion, pred[256,8192]{0,1:T(8,128)(4,1)S(1)} %compare_and_fusion), kind=kOutput, calls=%fused_computation.12 | convolution fusion | flops 2189426688 | bytes 38277120 | tf_op jit(solution)/shard_map/cond/branch_1_fun/hgnk,khd->hgnd/dot_general | solution.py:51
  200.5 15.0 %fusion.2 = f32[4,256]{1,0:T(4,128)S(1)} fusion(f32[8192,256,4]{1,0,2:T(8,128)} %get-tuple-element.97, f32[4,256]{1,0:T(4,128)S(1)} %broadcast_maximum_fusion, pred[256,8192]{0,1:T(8,128)(4,1)S(1)} %compare_and_fusion), kind=kLoop, calls=%fused_computation.4 | loop fusion | flops 41942016 | bytes 35659776 | tf_op jit(solution)/shard_map/cond/branch_1_fun/reduce_sum | solution.py:50
  215.5 0.2 fusion.19
  215.7 0.2 copy.17
  215.9 0.1 convert_element_type.20
  216.0 15.9 %all_to_all.16 = bf16[8,32,512]{2,1,0:T(8,128)(2,1)S(1)} all-to-all(bf16[8,32,512]{2,1,0:T(8,128)(2,1)S(1)} %convert_element_type.20), channel_id=1, replica_groups=mesh['ctx'=32,'head'=8] {'head'}, dimensions={0} | all-to-all | bytes 524288 | tf_op jit(solution)/shard_map/all_to_all | solution.py:80
  231.9 0.7 copy.20
  (4 shorter events, 0.0 us)
Async XLA Ops:
  6.5 80.5 %all-gather.4.cloned.1.call-start = ((), (), s32[]{:S(2)}) async-start(), calls=%async_computation.1 | async-start | bytes 2162688 | tf_op jit(solution)/shard_map/all_gather | solution.py:31
  7.3 157.5 %all-gather.6.cloned.1.call-start = ((), (), s32[]{:S(2)}) async-start(), calls=%async_computation.2 | async-start | bytes 2162688 | tf_op jit(solution)/shard_map/all_gather | solution.py:32
  164.7 20.5 %copy-start = (bf16[8192,1,128]{2,0,1:T(8,128)(2,1)S(1)}, bf16[8192,1,128]{2,0,1:T(8,128)(2,1)}, u32[]{:S(2)}) copy-start(bf16[8192,1,128]{2,0,1:T(8,128)(2,1)} %get-tuple-element.61) | copy-start | bytes 6291460 | tf_op jit(solution)/shard_map/cond
Sparse Core Ops, SparseCore 0:
  9.9 77.0 all-gather.3
  89.6 75.0 all-gather.5
where the time goes:
time: 240 us; the launch traced here: 239 us
  waiting for transfers between devices  120 us (50%)
  blocking collectives  53.8 us (22%)
  matrix products  30 us (12%)
  other arithmetic  20.9 us (9%)
  between operations  13.4 us (6%)
    all_gather x1, waiting for transfers between devices, attend(): value_piece = lax.all_gather(values, 'ctx', axis=0, tiled=True)  77.7 us
    all_gather x1, waiting for transfers between devices, attend(): key_piece = lax.all_gather(keys, 'ctx', axis=0, tiled=True)  41.1 us
    all_gather x1, blocking collectives, local(): all_ids = lax.all_gather(doc_ids, 'ctx', axis=0, tiled=True)  37.9 us
    all_to_all x1, blocking collectives, local(): lax.all_to_all(merged, 'head', split_axis=0, concat_axis=1, tiled=True)  15.9 us
    dot_general x1, matrix products, update(): jnp.einsum('hgnk,khd->hgnd', weights.astype(jnp.bfloat16), value_piece, p...  15.2 us
    reduce_sum x1, other arithmetic, update(): new_sum = jnp.sum(weights, axis=-1)  15 us
    dot_general x1, matrix products, update(): jnp.einsum('nhgd,khd->hgnk', grouped, key_piece, preferred_element_type=j...  14.7 us
    and x1, other arithmetic, update(): (key_pos[None, :] <= query_pos[:, None]) & (all_ids[None, :] == query_ids...  5.61 us
  transfers between devices with their start and end apart: 2, of which 2 were waited for; matrix products, arithmetic and copies ran while one was open for 0% of the time, Pallas kernels for 0%

commit v1 on v0

--- a/solution.py
+++ b/solution.py
@@ -29,7 +29,9 @@
     carried = tuple(initial)
     key_start = jnp.int32(0)
     key_piece = lax.all_gather(keys, "ctx", axis=0, tiled=True)
-    value_piece = lax.all_gather(values, "ctx", axis=0, tiled=True)
+    value_piece = jnp.concatenate(
+        lax.all_to_all(jnp.stack([values] * lax.axis_size("ctx")), "ctx", 0, 0), axis=0
+    )
     piece_len = key_piece.shape[0]
     key_pos = jnp.arange(piece_len, dtype=jnp.int32)
     updated = []

time: 240 us -> 178 us (0.74)
  waiting for transfers between devices: 120 us -> 0.71 us
  blocking collectives: 53.8 us -> 97.2 us
  starting transfers between devices: 0.04 us -> 11.9 us
  local copies, waits for them, and re-layouts: 1.12 us -> 3.77 us
    all_gather x1 -> x0, waiting for transfers between devices: 77.7 us -> none  [attend(): value_piece = lax.all_gather(values, 'ctx', axis=0, tiled=True)]
    all_gather x1, blocking collectives: 37.9 us -> 79.8 us  [local(): all_ids = lax.all_gather(doc_ids, 'ctx', axis=0, tiled=True)]
    all_gather x1, waiting for transfers between devices: 41.1 us -> 0.01 us  [attend(): key_piece = lax.all_gather(keys, 'ctx', axis=0, tiled=True)]
    all_to_all x0 -> x1, starting transfers between devices: none -> 11.9 us  [attend(): lax.all_to_all(jnp.stack([values] * lax.axis_size('ctx')), 'ctx', 0, 0)]
    another operation x0 -> x1, local copies, waits for them, and re-layouts: none -> 2.65 us  [attend(): jnp.stack([values] * lax.axis_size('ctx'))]
  transfers between devices with their start and end apart: 2 -> 2, of which waited for: 2 -> 0; matrix products, arithmetic and copies ran while one was open for 0% -> 1% of each run, Pallas kernels for 0% -> 0%
where the time goes in v1:
time: 178 us
  blocking collectives  97.2 us (55%)
  matrix products  30 us (17%)
  other arithmetic  20.9 us (12%)
  between operations  13.4 us (8%)
  starting transfers between devices  11.9 us (7%)
  local copies, waits for them, and re-layouts  3.77 us (2%)
    all_gather x1, blocking collectives, local(): all_ids = lax.all_gather(doc_ids, 'ctx', axis=0, tiled=True)  79.8 us
    all_to_all x1, blocking collectives, local(): lax.all_to_all(merged, 'head', split_axis=0, concat_axis=1, tiled=True)  17.4 us
    dot_general x1, matrix products, update(): jnp.einsum('hgnk,khd->hgnd', weights.astype(jnp.bfloat16), value_piece, p...  15.2 us
    reduce_sum x1, other arithmetic, update(): new_sum = jnp.sum(weights, axis=-1)  15 us
    dot_general x1, matrix products, update(): jnp.einsum('nhgd,khd->hgnk', grouped, key_piece, preferred_element_type=j...  14.7 us
    all_to_all x1, starting transfers between devices, attend(): lax.all_to_all(jnp.stack([values] * lax.axis_size('ctx')), 'ctx', 0, 0)  11.9 us
    and x1, other arithmetic, update(): (key_pos[None, :] <= query_pos[:, None]) & (all_ids[None, :] == query_ids...  5.61 us
  transfers between devices with their start and end apart: 2, of which 0 were waited for; matrix products, arithmetic and copies ran while one was open for 1% of the time, Pallas kernels for 0%

profile of v1, /device:TPU:1, one launch (start us, length us, event | category | flops | bytes accessed | tf_op | source)
XLA Modules:
  0.0 177.8 jit_solution(9789507428989010783)
XLA Ops:
  6.5 0.0 all-gather.3.cloned.1.call-start
  6.5 0.7 all-gather.3.cloned.1.call-update
  7.3 2.6 %stack.2 = bf16[32,256,1,128]{3,1,2,0:T(8,128)(2,1)} broadcast(bf16[256,128]{1,0:T(8,128)(2,1)} %bitcast.51), dimensions={1,3} | broadcast | bytes 2162688 | tf_op jit(solution)/shard_map/stack | solution.py:33
  9.9 11.9 %all-to-all-start = ((bf16[32,256,1,128]{3,1,2,0:T(8,128)(2,1)}), bf16[32,256,1,128]{3,1,2,0:T(8,128)(2,1)S(1)}, u32[]{:S(2)}, u32[]{:S(2)}) async-start(bf16[32,256,1,128]{3,1,2,0:T(8,128)(2,1)} %stack.2), calls=%async_computation | async-start | bytes 4194304 | tf_op jit(solution)/shard_map/all_to_all | solution.py:33
  21.8 79.8 %all-gather = s32[32,1,256]{2,1,0:T(1,128)S(1)} all-gather(s32[1,1,256]{2,1,0:T(1,128)} %bitcast.54), channel_id=1, replica_groups=mesh['ctx'=32,'head'=8] {'ctx'}, dimensions={0}, use_global_device_ids=true | all-gather | bytes 33792 | tf_op jit(solution)/shard_map/all_gather | solution.py:79
  101.6 0.0 all-gather.3.cloned.1.call-done
  101.6 0.0 all-to-all-done
  101.6 50.7 %conditional.1 = (f32[1,4,256]{2,1,0:T(4,128)S(1)}, f32[1,4,256,128]{3,2,1,0:T(8,128)S(1)}) conditional(s32[]{:T(128)} %convert_element_type.17, () %tuple.16, (s32[8192]{0:T(1024)S(1)}, s32[]{:T(128)}, s32[256]{0:T(256)S(1)}, s32[8192]{0:T(1024)S(1)}, bf16[8192,1,128]{2,0,1:T(8,128)(2,1)}, /*index=5*/bf16[256,4,128]{2,1,0:T(4,128)(2,1)}, ...), branch_computations={%region_0.0_spmd, %region_1.4_spmd} | conditional | flops 4410309632 | bytes 114128952 | solution.py:64
  101.6 0.1 dynamic_slice.4
  101.7 5.6 %compare_and_fusion = pred[256,8192]{0,1:T(8,128)(4,1)S(1)} fusion(s32[256]{0:T(256)S(1)} %dynamic_slice.4, s32[256]{0:T(256)S(1)} %broadcast_add_fusion, s32[8192]{0:T(1024)S(1)} %get-tuple-element.59, s32[8192]{0:T(1024)S(1)} %get-tuple-element.56), kind=kLoop, calls=%fused_computation.8 | loop fusion | flops 6291456 | bytes 2164736 | tf_op jit(solution)/shard_map/cond/branch_1_fun/and | solution.py:46
  107.3 14.7 %fusion = (f32[4,256]{1,0:T(4,128)S(1)}, f32[8192,256,4]{1,0,2:T(8,128)}) fusion(pred[256,8192]{0,1:T(8,128)(4,1)S(1)} %compare_and_fusion, bf16[256,4,128]{2,1,0:T(4,128)(2,1)} %get-tuple-element.95, bf16[8192,1,128]{2,0,1:T(8,128)(2,1)} %get-tuple-element.60), kind=kOutput, calls=%fused_computation.2 | convolution fusion | flops 2172648448 | bytes 38014976 | tf_op jit(solution)/shard_map/cond/branch_1_fun/nhgd,khd->hgnk/dot_general | solution.py:43
  122.0 15.2 %fusion.9 = f32[1,4,256,128]{3,2,1,0:T(8,128)S(1)} fusion(bf16[8192,128,1]{1,0,2:T(8,128)(2,1)S(1)} %bitcast.48, f32[8192,256,4]{1,0,2:T(8,128)} %get-tuple-element.98, f32[4,256]{1,0:T(4,128)S(1)} %broadcast_maximum_fusion, pred[256,8192]{0,1:T(8,128)(4,1)S(1)} %compare_and_fusion), kind=kOutput, calls=%fused_computation.11 | convolution fusion | flops 2189426688 | bytes 38277120 | tf_op jit(solution)/shard_map/cond/branch_1_fun/hgnk,khd->hgnd/dot_general | solution.py:53
  137.3 15.0 %fusion.2 = f32[4,256]{1,0:T(4,128)S(1)} fusion(f32[8192,256,4]{1,0,2:T(8,128)} %get-tuple-element.98, f32[4,256]{1,0:T(4,128)S(1)} %broadcast_maximum_fusion, pred[256,8192]{0,1:T(8,128)(4,1)S(1)} %compare_and_fusion), kind=kLoop, calls=%fused_computation.4 | loop fusion | flops 41942016 | bytes 35659776 | tf_op jit(solution)/shard_map/cond/branch_1_fun/reduce_sum | solution.py:52
  152.3 0.2 fusion.16
  152.5 0.2 copy.18
  152.8 0.1 convert_element_type.20
  152.9 17.4 %all_to_all.21 = bf16[8,32,512]{2,1,0:T(8,128)(2,1)S(1)} all-to-all(bf16[8,32,512]{2,1,0:T(8,128)(2,1)S(1)} %convert_element_type.20), channel_id=1, replica_groups=mesh['ctx'=32,'head'=8] {'head'}, dimensions={0} | all-to-all | bytes 524288 | tf_op jit(solution)/shard_map/all_to_all | solution.py:82
  170.2 0.7 copy.21
  (4 shorter events, 0.0 us)
Async XLA Ops:
  6.5 95.0 %all-gather.3.cloned.1.call-start = ((), (), s32[]{:S(2)}) async-start(), calls=%async_computation.2 | async-start | bytes 2162688 | tf_op jit(solution)/shard_map/all_gather | solution.py:31
  9.9 91.7 %all-to-all-start = ((bf16[32,256,1,128]{3,1,2,0:T(8,128)(2,1)}), bf16[32,256,1,128]{3,1,2,0:T(8,128)(2,1)S(1)}, u32[]{:S(2)}, u32[]{:S(2)}) async-start(bf16[32,256,1,128]{3,1,2,0:T(8,128)(2,1)} %stack.2), calls=%async_computation | async-start | bytes 4194304 | tf_op jit(solution)/shard_map/all_to_all | solution.py:33
Sparse Core Ops, SparseCore 0:
  9.9 83.0 all-gather.2
